TPU v7x, 32 devices: a whole 2x2x4 slice. The times are simulated.
32 devices in a mesh: dp: 4 (over z), row: 4 (over y, x), col: 2 (over core).
Axes of the slice: x: 2, y: 2, z: 4, core: 2. Of those that a mesh axis runs over, the one named last changes fastest.
Arguments:
- tokens: bfloat16 [8, 2048, 768], P(('dp', 'col'), 'row'), may hold values from -6 to 6
- cotangent: bfloat16 [8, 2048, 768], P(('dp', 'col'), 'row'), may hold values from -6 to 6
- timesteps: int32 [8], P(('dp', 'col')), may hold values from 0 to 999
- prefix_len: int32 [8], P(('dp', 'col')), may hold values from 204 to 1024, as said below
- time_table: bfloat16 [1000, 768], P('col'), may hold values from -3 to 3
- ln1_gain: float32 [768], replicated, may hold values from 0.25 to 1.75
- ln1_bias: float32 [768], replicated, may hold values from -3 to 3
- w_qkv: bfloat16 [768, 3, 768], P('col', None, 'row'), may hold values from -0.3125 to 0.3125
- w_out: bfloat16 [768, 768], P('col', 'row'), may hold values from -1.75 to 1.75
- out_bias: float32 [768], replicated, may hold values from -3 to 3
- ln2_gain: float32 [768], replicated, may hold values from 0.25 to 1.75
- ln2_bias: float32 [768], replicated, may hold values from -3 to 3
- w_up: bfloat16 [768, 3072], P('col', 'row'), may hold values from -0.21875 to 0.21875
- up_bias: float32 [3072], P('row'), may hold values from -3 to 3
- w_down: bfloat16 [768, 3072], P('col', 'row'), may hold values from -0.109375 to 0.109375
- down_bias: float32 [768], replicated, may hold values from -4 to 4
Outputs:
- layer_out: bfloat16 [8, 2048, 768], P(('dp', 'col'), 'row')
- tokens_grad: float32 [8, 2048, 768], P(('dp', 'col'), 'row')
- table_grad: float32 [1000, 768], P('col')
- ln1_gain_grad: float32 [768], replicated
- ln1_bias_grad: float32 [768], replicated
- qkv_grad: float32 [768, 3, 768], P('col', None, 'row')
- out_grad: float32 [768, 768], P('col', 'row')
- out_bias_grad: float32 [768], replicated
- ln2_gain_grad: float32 [768], replicated
- ln2_bias_grad: float32 [768], replicated
- up_grad: float32 [768, 3072], P('col', 'row')
- up_bias_grad: float32 [3072], P('row')
- down_grad: float32 [768, 3072], P('col', 'row')
- down_bias_grad: float32 [768], replicated
Inputs may be any that keep to these rules, and one draw needn't show every extreme that they name: `prefix_len`: each sequence's prefix length lies between 204 and 1024, and some sequence takes each end.
All inputs are finite; a program needn't handle non-finite values.
Results may differ from a plain program's by a relative error of at most 0.02.
Values may be sent and summed in bfloat16 or wider, within the bound.
A program may use at most 128 MiB of HBM per device.

v0:
```python
import jax
import jax.numpy as jnp
from jax import lax
from jax.sharding import PartitionSpec as P

HD = 64
norm_eps = 1e-05
masked_score = -1e30


def gelu_exact(values):
    return jax.nn.gelu(values, approximate=False)


def gather_rows(values):
    return lax.all_gather(values, "row", axis=1, tiled=True)


def scatter_rows(values):
    return lax.psum_scatter(
        values.astype(jnp.bfloat16), "row", scatter_dimension=1, tiled=True
    ).astype(jnp.float32)


def gather_grads(values):
    return lax.all_gather(values, "row", axis=1, tiled=True)


def scatter_grads(values):
    return lax.psum_scatter(
        values.astype(jnp.bfloat16), "row", scatter_dimension=1, tiled=True
    ).astype(jnp.float32)


def norm_forward(hidden, gain_vec, bias_vec):
    width = hidden.shape[-1]
    average = jnp.sum(hidden, axis=-1, keepdims=True) / width
    variance = jnp.sum(hidden * hidden, axis=-1, keepdims=True) / width - average * average
    inverse = lax.rsqrt(variance + norm_eps)
    centred = (hidden - average) * inverse
    return (centred * gain_vec + bias_vec, centred, inverse)


def norm_backward(grad_out, centred, inverse, gain_vec):
    width = grad_out.shape[-1]
    scaled = grad_out * gain_vec
    first_mean = jnp.sum(scaled, axis=-1, keepdims=True) / width
    second_mean = jnp.sum(scaled * centred, axis=-1, keepdims=True) / width
    grad_in = inverse * (scaled - first_mean - centred * second_mean)
    return (grad_in, jnp.sum(grad_out * centred, axis=(0, 1)), jnp.sum(grad_out, axis=(0, 1)))


def attend_forward(queries, key_rows, values, prefix):
    length = queries.shape[0]
    block_rows = min(512, length)
    score_scale = queries.shape[2] ** (-0.5)
    key_pos = jnp.arange(length, dtype=jnp.int32)

    def one_block(block_index):
        row_start = block_index * block_rows
        query_blk = lax.dynamic_slice_in_dim(queries, row_start, block_rows, 0)
        scores = (
            jnp.einsum("qhd,khd->hqk", query_blk, key_rows, preferred_element_type=jnp.float32)
            * score_scale
        )
        query_pos = row_start + jnp.arange(block_rows, dtype=jnp.int32)
        allowed = (key_pos[None, :] <= query_pos[:, None]) | (key_pos[None, :] < prefix)
        scores = jnp.where(allowed[None], scores, masked_score)
        row_max = jnp.max(scores, axis=2, keepdims=True)
        exponent = jnp.exp(scores - row_max)
        row_total = jnp.sum(exponent, axis=2, keepdims=True)
        soft_low = (exponent / row_total).astype(jnp.bfloat16)
        mixed_blk = jnp.einsum("hqk,khd->qhd", soft_low, values, preferred_element_type=jnp.float32)
        return (mixed_blk, (row_max + jnp.log(row_total))[:, :, 0])

    mixed, logsums = lax.map(one_block, jnp.arange(length // block_rows, dtype=jnp.int32))
    return (mixed.reshape(queries.shape), logsums)


def attend_backward(queries, key_rows, values, mixed, logsums, grad_mixed, prefix):
    length = queries.shape[0]
    block_rows = min(512, length)
    score_scale = queries.shape[2] ** (-0.5)
    key_pos = jnp.arange(length, dtype=jnp.int32)
    delta = jnp.sum(grad_mixed.astype(jnp.float32) * mixed, axis=2)

    def one_block(grads_carry, block_index):
        grad_keys, grad_values = grads_carry
        row_start = block_index * block_rows
        query_blk = lax.dynamic_slice_in_dim(queries, row_start, block_rows, 0)
        grad_blk = lax.dynamic_slice_in_dim(grad_mixed, row_start, block_rows, 0)
        delta_blk = lax.dynamic_slice_in_dim(delta, row_start, block_rows, 0)
        scores = (
            jnp.einsum("qhd,khd->hqk", query_blk, key_rows, preferred_element_type=jnp.float32)
            * score_scale
        )
        query_pos = row_start + jnp.arange(block_rows, dtype=jnp.int32)
        allowed = (key_pos[None, :] <= query_pos[:, None]) | (key_pos[None, :] < prefix)
        scores = jnp.where(allowed[None], scores, masked_score)
        weights_soft = jnp.exp(scores - logsums[block_index][:, :, None])
        grad_soft = jnp.einsum("qhd,khd->hqk", grad_blk, values, preferred_element_type=jnp.float32)
        grad_scores = (weights_soft * (grad_soft - delta_blk.T[:, :, None])).astype(jnp.bfloat16)
        grad_query = (
            jnp.einsum("hqk,khd->qhd", grad_scores, key_rows, preferred_element_type=jnp.float32)
            * score_scale
        )
        grad_keys = (
            grad_keys
            + jnp.einsum("hqk,qhd->khd", grad_scores, query_blk, preferred_element_type=jnp.float32)
            * score_scale
        )
        grad_values = grad_values + jnp.einsum(
            "hqk,qhd->khd",
            weights_soft.astype(jnp.bfloat16),
            grad_blk,
            preferred_element_type=jnp.float32,
        )
        return ((grad_keys, grad_values), grad_query)

    zero_grads = jnp.zeros(key_rows.shape, jnp.float32)
    final_grads, grad_queries = lax.scan(
        one_block, (zero_grads, zero_grads), jnp.arange(length // block_rows, dtype=jnp.int32)
    )
    return jnp.stack([grad_queries.reshape(key_rows.shape), final_grads[0], final_grads[1]], axis=1)


def body(
    tokens,
    cotangent,
    timesteps,
    prefix_len,
    time_table,
    ln1_gain,
    ln1_bias,
    w_qkv,
    w_out,
    out_bias,
    ln2_gain,
    ln2_bias,
    w_up,
    up_bias,
    w_down,
    down_bias,
):
    highest = lax.Precision.HIGHEST
    qkv_full, out_full, up_full, down_full, table_full = (
        lax.all_gather(w_qkv, "col", axis=0, tiled=True),
        lax.all_gather(w_out, "col", axis=0, tiled=True),
        lax.all_gather(w_up, "col", axis=0, tiled=True),
        lax.all_gather(w_down, "col", axis=0, tiled=True),
        lax.all_gather(time_table, "col", axis=0, tiled=True),
    )
    seq_count = tokens.shape[0]
    width_heads = qkv_full.shape[2]
    heads_local = width_heads // HD
    picked = (
        timesteps[:, None] == jnp.arange(table_full.shape[0], dtype=jnp.int32)[None, :]
    ).astype(jnp.float32)
    embed_rows = jnp.dot(picked, table_full.astype(jnp.float32), precision=highest)

    def sequence_forward(seq_item):
        parts_seq, prefix = seq_item
        return attend_forward(parts_seq[:, 0], parts_seq[:, 1], parts_seq[:, 2], prefix)

    def forward_pass(tokens_in):
        hidden0 = tokens_in.astype(jnp.float32) + embed_rows[:, None, :]
        normed1, centred1, inverse1 = norm_forward(hidden0, ln1_gain, ln1_bias)
        full_one = gather_rows(normed1.astype(jnp.bfloat16))
        length = full_one.shape[1]
        project = jnp.einsum(
            "std,dkh->stkh", full_one, qkv_full, preferred_element_type=jnp.float32
        ).astype(jnp.bfloat16)
        parts = project.reshape(seq_count, length, 3, heads_local, HD)
        mixed, logsums = lax.map(sequence_forward, (parts, prefix_len))
        weighted = mixed.reshape(seq_count, length, width_heads).astype(jnp.bfloat16)
        branch = scatter_rows(
            jnp.einsum("sth,dh->std", weighted, out_full, preferred_element_type=jnp.float32)
        )
        hidden1 = hidden0 + (branch + out_bias)
        normed2, centred2, inverse2 = norm_forward(hidden1, ln2_gain, ln2_bias)
        full_two = gather_rows(normed2.astype(jnp.bfloat16))
        inner = (
            jnp.einsum("std,df->stf", full_two, up_full, preferred_element_type=jnp.float32)
            + up_bias
        )
        active = gelu_exact(inner).astype(jnp.bfloat16)
        result = hidden1 + (
            scatter_rows(
                jnp.einsum("stf,df->std", active, down_full, preferred_element_type=jnp.float32)
            )
            + down_bias
        )
        saved = (
            full_one,
            centred1,
            inverse1,
            parts,
            mixed,
            logsums,
            weighted,
            centred2,
            inverse2,
            full_two,
            inner,
            active,
        )
        return (result, saved)

    result, saved = forward_pass(tokens)
    (
        full_one,
        centred1,
        inverse1,
        parts,
        mixed,
        logsums,
        weighted,
        centred2,
        inverse2,
        full_two,
        inner,
        active,
    ) = saved
    length = full_one.shape[1]
    grad_full = gather_grads(cotangent)
    down_grad_full = jnp.einsum(
        "std,stf->df", grad_full, active, preferred_element_type=jnp.float32
    )
    grad_active = jnp.einsum(
        "std,df->stf", grad_full, down_full, preferred_element_type=jnp.float32
    )
    unused_out, gelu_back = jax.vjp(gelu_exact, inner)
    grad_inner = gelu_back(grad_active)[0]
    inner_low = grad_inner.astype(jnp.bfloat16)
    up_grad_full = jnp.einsum(
        "std,stf->df", full_two, inner_low, preferred_element_type=jnp.float32
    )
    grad_normed2 = scatter_grads(
        jnp.einsum("stf,df->std", inner_low, up_full, preferred_element_type=jnp.float32)
    )
    grad_norm_two, ln2_gain_part, ln2_bias_part = norm_backward(
        grad_normed2, centred2, inverse2, ln2_gain
    )
    grad_hidden1 = cotangent.astype(jnp.float32) + grad_norm_two
    grad_branch_full = gather_grads(grad_hidden1.astype(jnp.bfloat16))
    out_grad_full = jnp.einsum(
        "std,sth->dh", grad_branch_full, weighted, preferred_element_type=jnp.float32
    )
    grad_weighted = jnp.einsum(
        "std,dh->sth", grad_branch_full, out_full, preferred_element_type=jnp.float32
    ).astype(jnp.bfloat16)

    def sequence_backward(seq_item):
        parts_seq, mixed_seq, logsum_seq, grad_seq, prefix = seq_item
        return attend_backward(
            parts_seq[:, 0],
            parts_seq[:, 1],
            parts_seq[:, 2],
            mixed_seq,
            logsum_seq,
            grad_seq,
            prefix,
        )

    grad_parts = lax.map(
        sequence_backward,
        (
            parts,
            mixed,
            logsums,
            grad_weighted.reshape(seq_count, length, heads_local, HD),
            prefix_len,
        ),
    )
    grad_project = grad_parts.reshape(seq_count, length, 3, width_heads).astype(jnp.bfloat16)
    qkv_grad_full = jnp.einsum(
        "std,stkh->dkh", full_one, grad_project, preferred_element_type=jnp.float32
    )
    grad_normed1 = scatter_grads(
        jnp.einsum("stkh,dkh->std", grad_project, qkv_full, preferred_element_type=jnp.float32)
    )
    grad_norm_one, ln1_gain_part, ln1_bias_part = norm_backward(
        grad_normed1, centred1, inverse1, ln1_gain
    )
    grad_hidden0 = grad_hidden1 + grad_norm_one
    seq_sums = jnp.sum(grad_hidden0, axis=1)
    table_grad_full = jnp.einsum("sn,sd->nd", picked, seq_sums, precision=highest)
    vectors = lax.psum(
        (
            ln1_gain_part,
            ln1_bias_part,
            jnp.sum(grad_hidden1, axis=(0, 1)),
            ln2_gain_part,
            ln2_bias_part,
            jnp.sum(cotangent.astype(jnp.float32), axis=(0, 1)),
        ),
        ("dp", "row", "col"),
    )
    up_bias_grad = lax.psum(jnp.sum(grad_inner, axis=(0, 1)), ("dp", "col"))
    weights_full = (qkv_grad_full, out_grad_full, up_grad_full, down_grad_full)
    blocks = (
        lax.psum_scatter(
            weights_full[0].astype(jnp.bfloat16), "col", scatter_dimension=0, tiled=True
        ).astype(jnp.float32),
        lax.psum_scatter(
            weights_full[1].astype(jnp.bfloat16), "col", scatter_dimension=0, tiled=True
        ).astype(jnp.float32),
        lax.psum_scatter(
            weights_full[2].astype(jnp.bfloat16), "col", scatter_dimension=0, tiled=True
        ).astype(jnp.float32),
        lax.psum_scatter(
            weights_full[3].astype(jnp.bfloat16), "col", scatter_dimension=0, tiled=True
        ).astype(jnp.float32),
        lax.psum_scatter(
            table_grad_full.astype(jnp.bfloat16), "col", scatter_dimension=0, tiled=True
        ).astype(jnp.float32),
    )
    weight_blocks = (blocks[0], blocks[1], blocks[2], blocks[3])
    weight_blocks = (
        lax.psum(blocks[0].astype(jnp.bfloat16), "dp").astype(jnp.float32),
        lax.psum(blocks[1].astype(jnp.bfloat16), "dp").astype(jnp.float32),
        lax.psum(blocks[2].astype(jnp.bfloat16), "dp").astype(jnp.float32),
        lax.psum(blocks[3].astype(jnp.bfloat16), "dp").astype(jnp.float32),
    )
    table_block = lax.psum(blocks[4].astype(jnp.bfloat16), ("dp", "row")).astype(jnp.float32)
    return (
        result.astype(jnp.bfloat16),
        grad_hidden0,
        table_block,
        vectors[0],
        vectors[1],
        weight_blocks[0],
        weight_blocks[1],
        vectors[2],
        vectors[3],
        vectors[4],
        weight_blocks[2],
        up_bias_grad,
        weight_blocks[3],
        vectors[5],
    )


def solution(mesh):
    placed = (
        P(("dp", "col"), "row", None),
        P(("dp", "col"), "row", None),
        P(("dp", "col")),
        P(("dp", "col")),
        P("col", None),
        P(),
        P(),
        P("col", None, "row"),
        P("col", "row"),
        P(),
        P(),
        P(),
        P("col", "row"),
        P("row"),
        P("col", "row"),
        P(),
    )
    return jax.shard_map(
        body,
        mesh=mesh,
        in_specs=placed,
        out_specs=(
            P(("dp", "col"), "row", None),
            P(("dp", "col"), "row", None),
            P("col", None),
            P(),
            P(),
            P("col", None, "row"),
            P("col", "row"),
            P(),
            P(),
            P(),
            P("col", "row"),
            P("row"),
            P("col", "row"),
            P(),
        ),
        check_vma=False,
    )
```

profile of v0, /device:TPU:0, one launch (start us, length us, event | category | flops | bytes accessed | tf_op | source)
XLA Modules:
  0.0 882.5 jit_solution(11795420427352458064)
XLA Ops:
  8.7 13.4 %all-gather.21.cloned.1.call-done = bf16[2,500,768]{2,1,0:T(8,128)(2,1)} async-done(((bf16[1,500,768]{2,1,0:T(8,128)(2,1)}), bf16[2,500,768]{2,1,0:T(8,128)(2,1)}) %all-gather.21.cloned.1.call-update) | async-done | bytes 1536016 | tf_op jit(solution)/shard_map/all_gather | solution.py:151
  30.4 40.8 %all-gather.9.cloned.1.call-done = bf16[1,2048,768]{2,1,0:T(8,128)(2,1)} async-done(((bf16[1,512,768]{2,1,0:T(8,128)(2,1)}), bf16[1,2048,768]{2,1,0:T(8,128)(2,1)}) %all-gather.9.cloned.1.call-update) | async-done | bytes 3145744 | tf_op jit(solution)/shard_map/all_gather | solution.py:16
  71.2 3.9 fusion.62
  75.7 91.3 %while.50 = (s32[]{:T(128)}, f32[4,512,3,64]{1,3,2,0:T(8,128)}, f32[4,3,512]{2,1,0:T(4,128)S(1)}, s32[4]{0:T(128)S(1)}, s32[]{:T(128)}, /*index=5*/bf16[2048,3,6...) while((s32[]{:T(128)}, f32[4,512,3,64]{1,3,2,0:T(8,128)}, ...), condition=%wide.region_5.6_spmd.clone.clone.clone, body=%wide.region_2.5_spmd.clone.clone.sunk.clone | while | flops 845153280 | bytes 44169396 | solution.py:76
  78.4 6.0 fusion.182
  84.4 6.8 fusion.183
  91.2 7.4 fusion.184
  101.2 6.0 fusion.182
  107.2 6.8 fusion.183
  114.0 7.4 fusion.184
  124.1 6.0 fusion.182
  130.1 6.8 fusion.183
  136.8 7.4 fusion.184
  146.9 6.0 fusion.182
  152.9 6.8 fusion.183
  159.6 7.3 fusion.184
  174.1 43.3 %reduce-scatter.17.cloned.1.call-done = bf16[1,512,768]{2,1,0:T(8,128)(2,1)} async-done(((bf16[1,2048,768]{2,1,0:T(8,128)(2,1)}), bf16[1,512,768]{2,1,0:T(8,128)(2,1)}) %reduce-scatter.17.cloned.1.call-update) | async-done | bytes 786448 | tf_op jit(solution)/shard_map/reduce_scatter | solution.py:20
  223.0 5.0 all-gather.13.cloned.1.call-done
  228.0 47.4 %all-gather.11.cloned.1.call-done = bf16[1,2048,768]{2,1,0:T(8,128)(2,1)} async-done(((bf16[1,512,768]{2,1,0:T(8,128)(2,1)}), bf16[1,2048,768]{2,1,0:T(8,128)(2,1)}) %all-gather.11.cloned.1.call-update) | async-done | bytes 3145744 | tf_op jit(solution)/shard_map/all_gather | solution.py:16
  275.4 19.0 %multiply_convert_fusion.1 = (bf16[2048,768]{1,0:T(8,128)(2,1)}, f32[2048,768]{1,0:T(8,128)}, f32[2048,768]{1,0:T(8,128)}) fusion(f32[768]{0:T(1024)S(1)} %copy-done.41, bf16[768,768]{1,0:T(8,128)(2,1)} %all-gather.13.cloned.1.call-done, bf16[1,2048,768]{2,1,0:T(8,128)(2,1)} %all-gather.11.cloned.1.call-done), kind=kOutput, calls=%fused_computation.54 | convolution fusion | flops 2519728128 | bytes 20057088 | tf_op jit(solution)/shard_map/std,df->stf/dot_general | solution.py:183
  294.4 38.7 %all-gather.17.cloned.1.call-done = bf16[1,2048,768]{2,1,0:T(8,128)(2,1)} async-done(((bf16[1,512,768]{2,1,0:T(8,128)(2,1)}), bf16[1,2048,768]{2,1,0:T(8,128)(2,1)}) %all-gather.17.cloned.1.call-update) | async-done | bytes 3145744 | tf_op jit(solution)/shard_map/all_gather | solution.py:26
  333.1 11.2 %fusion.112 = (f32[768]{0:T(1024)}, bf16[2048,768]{1,0:T(8,128)(2,1)S(1)}) fusion(f32[2048,768]{1,0:T(8,128)} %get-tuple-element.398, bf16[768,768]{1,0:T(8,128)(2,1)} %all-gather.15.cloned.1.call-done, bf16[1,2048,768]{2,1,0:T(8,128)(2,1)} %all-gather.17.cloned.1.call-done, f32[2048,768]{1,0:T(8,128)} %get-tuple-element.410, f32[768]{0:T(1024)S(1)} %copy-done.41), kind=kOutput, calls=%fused_computation.153 | convolution fusion | flops 2441084160 | bytes 20060160 | tf_op jit(solution)/shard_map/std,df->stf/dot_general | solution.py:229
  345.9 4.0 fusion.66
  350.2 6.6 fusion.65
  356.9 37.2 %reduce-scatter.21.cloned.1.call-done = bf16[1,512,768]{2,1,0:T(8,128)(2,1)} async-done(((bf16[1,2048,768]{2,1,0:T(8,128)(2,1)}), bf16[1,512,768]{2,1,0:T(8,128)(2,1)}) %reduce-scatter.21.cloned.1.call-update) | async-done | bytes 786448 | tf_op jit(solution)/shard_map/reduce_scatter | solution.py:30
  396.8 44.2 %reduce-scatter.19.cloned.1.call-done = bf16[1,512,768]{2,1,0:T(8,128)(2,1)} async-done(((bf16[1,2048,768]{2,1,0:T(8,128)(2,1)}), bf16[1,512,768]{2,1,0:T(8,128)(2,1)}) %reduce-scatter.19.cloned.1.call-update) | async-done | bytes 786448 | tf_op jit(solution)/shard_map/reduce_scatter | solution.py:20
  441.1 4.2 fusion.108
  448.5 6.5 fusion.100
  457.5 34.1 %all-gather.19.cloned.1.call-done = bf16[1,2048,768]{2,1,0:T(8,128)(2,1)} async-done(((bf16[1,512,768]{2,1,0:T(8,128)(2,1)}), bf16[1,2048,768]{2,1,0:T(8,128)(2,1)}) %all-gather.19.cloned.1.call-update) | async-done | bytes 3145744 | tf_op jit(solution)/shard_map/all_gather | solution.py:26
  491.6 3.9 fusion.68
  501.2 87.8 %while.51 = (s32[]{:T(128)}, f32[2048,3,64]{0,2,1:T(8,128)S(1)}, f32[2048,3,64]{0,2,1:T(8,128)}, bf16[4,512,3,64]{1,3,2,0:T(8,128)(2,1)}, s32[4]{0:T(128)S(1)}, ...) while((s32[]{:T(128)}, f32[2048,3,64]{0,2,1:T(8,128)S(1)}, ...), condition=%wide.region_15.16_spmd.clone.clone.clone, body=%wide.region_14.15_spmd.clone.clone.sunk.clone | while | flops 2048887296 | bytes 79087952 | solution.py:121
  508.2 5.8 fusion.198
  514.0 5.6 multiply_convert_fusion.5
  529.5 6.4 fusion.198
  535.9 5.6 multiply_convert_fusion.5
  551.5 6.4 fusion.198
  557.9 5.6 multiply_convert_fusion.5
  573.4 6.4 fusion.198
  579.8 5.6 multiply_convert_fusion.5
  601.8 6.8 fusion.92
  608.6 4.0 fusion.67
  618.8 10.4 %reduce-scatter.25.cloned.1.call-done = bf16[384,768]{1,0:T(8,128)(2,1)} async-done(((bf16[768,768]{1,0:T(8,128)(2,1)}), bf16[384,768]{1,0:T(8,128)(2,1)}) %reduce-scatter.25.cloned.1.call-update) | async-done | bytes 589840 | tf_op jit(solution)/shard_map/reduce_scatter | solution.py:308
  629.3 48.0 %reduce-scatter.23.cloned.1.call-done = bf16[1,512,768]{2,1,0:T(8,128)(2,1)} async-done(((bf16[1,2048,768]{2,1,0:T(8,128)(2,1)}), bf16[1,512,768]{2,1,0:T(8,128)(2,1)}) %reduce-scatter.23.cloned.1.call-update) | async-done | bytes 786448 | tf_op jit(solution)/shard_map/reduce_scatter | solution.py:30
  682.5 4.4 fusion.4
  693.0 18.3 %psum.93 = f32[768]{0:T(1024)} all-reduce(f32[768]{0:T(1024)S(1)} %copy-done.37), channel_id=1, replica_groups=mesh['dp'=4,'row'=4,'col'=2] {'dp','col'}, use_global_device_ids=true, to_apply=%region_39.40 | all-reduce | flops 768 | bytes 6144 | tf_op jit(solution)/shard_map/psum | solution.py:299
  711.3 46.5 %all-reduce.9.cloned.1.call-done = (bf16[384,768]{0,1:T(8,128)(2,1)}, bf16[384,3,192]{0,2,1:T(8,128)(2,1)}, bf16[384,192]{0,1:T(8,128)(2,1)}, bf16[384,768]{1,0:T(8,128)(2,1)}) async-done(((bf16[384,768]{0,1:T(8,128)(2,1)}, bf16[384,3,192]{0,2,1:T(8,128)(2,1)}, bf16[384,192]{0,1:T(8,128)(2,1)}, bf16[384,768]{1,0:T(8,128)(2,1)}), (bf16[384,768]{0,1:T(8,128)(2,1)}, bf16[384,3,192]{0,2,1:T(8,128)(2,1)}, ...) | async-done | bytes 1769488 | tf_op jit(solution)/shard_map/psum | solution.py:323
  765.0 40.0 %all-reduce.2 = (f32[768]{0:T(1024)}, f32[768]{0:T(1024)}, f32[768]{0:T(1024)}, f32[768]{0:T(1024)}, f32[768]{0:T(1024)}, /*index=5*/f32[768]{0:T(1024)}) all-reduce(f32[768]{0:T(1024)S(1)} %get-tuple-element.333, f32[768]{0:T(1024)S(1)} %get-tuple-element.342, ...), channel_id=1, replica_groups=mesh['dp'=4,'row'=4,'col'=2] {'dp','row','col'}, use_global_device_ids=true, to_apply=%region_23.24 | all-reduce | flops 4608 | bytes 36864 | tf_op jit(solution)/shard_map/psum | solution.py:288
  804.9 68.4 %all-reduce.7.cloned.1.call-done = bf16[500,768]{1,0:T(8,128)(2,1)} async-done(((bf16[500,768]{1,0:T(8,128)(2,1)}), bf16[500,768]{1,0:T(8,128)(2,1)}) %all-reduce.7.cloned.1.call-update) | async-done | bytes 768016 | tf_op jit(solution)/shard_map/psum | solution.py:325
  (259 shorter events, 114.1 us)
Async XLA Ops:
  7.2 17.0 %copy-start = (bf16[1,512,768]{2,1,0:T(8,128)(2,1)S(1)}, bf16[1,512,768]{2,1,0:T(8,128)(2,1)}, u32[]{:S(2)}) copy-start(bf16[1,512,768]{2,1,0:T(8,128)(2,1)} %param.20) | copy-start | bytes 2359300
  7.2 17.4 %copy-start.24 = (f32[768]{0:T(1024)S(1)}, f32[768]{0:T(1024)}, u32[]{:S(2)}) copy-start(f32[768]{0:T(1024)} %param.25) | copy-start | bytes 9220
  7.2 17.4 %copy-start.34 = (f32[768]{0:T(1024)S(1)}, f32[768]{0:T(1024)}, u32[]{:S(2)}) copy-start(f32[768]{0:T(1024)} %param.26) | copy-start | bytes 9220
  7.2 14.9 %all-gather.21.cloned.1.call-start = ((), (), s32[]{:S(2)}) async-start(), calls=%async_computation.20 | async-start | bytes 2322432 | tf_op jit(solution)/shard_map/all_gather | solution.py:151
  7.9 63.2 %all-gather.9.cloned.1.call-start = ((), (), s32[]{:S(2)}) async-start(), calls=%async_computation.8 | async-start | bytes 3932160 | tf_op jit(solution)/shard_map/all_gather | solution.py:16
  8.7 17.3 %copy-start.21 = (bf16[384,192]{0,1:T(8,128)(2,1)S(1)}, bf16[384,192]{0,1:T(8,128)(2,1)}, u32[]{:S(2)}) copy-start(bf16[384,192]{0,1:T(8,128)(2,1)} %param.28) | copy-start | bytes 442372
  24.1 416.9 %copy-start.19 = (f32[768]{0:T(1024)}, f32[768]{0:T(1024)S(1)}, u32[]{:S(2)}) copy-start(f32[768]{0:T(1024)S(1)} %convolution_reduce_fusion) | copy-start | bytes 9220
  24.6 50.5 %copy-start.26 = (f32[512]{0:T(512)}, f32[512]{0:T(512)S(1)}, u32[]{:S(2)}) copy-start(f32[512]{0:T(512)S(1)} %get-tuple-element.408) | copy-start | bytes 6148
  24.6 50.5 %copy-start.28 = (f32[512]{0:T(512)}, f32[512]{0:T(512)S(1)}, u32[]{:S(2)}) copy-start(f32[512]{0:T(512)S(1)} %get-tuple-element.409) | copy-start | bytes 6148
  25.9 191.5 %reduce-scatter.17.cloned.1.call-start = ((), (), s32[]{:S(2)}) async-start(), calls=%async_computation.9 | async-start | bytes 3932160 | tf_op jit(solution)/shard_map/reduce_scatter | solution.py:20
  30.4 44.7 %copy-start.13 = (bf16[768,3,192]{0,2,1:T(8,128)(2,1)}, bf16[768,3,192]{0,2,1:T(8,128)(2,1)S(1)}, u32[]{:S(2)}) copy-start(bf16[768,3,192]{0,2,1:T(8,128)(2,1)S(1)} %all_gather.29) | copy-start | bytes 2654212
  173.2 44.2 %copy-start.22 = (f32[768]{0:T(1024)S(1)}, f32[768]{0:T(1024)}, u32[]{:S(2)}) copy-start(f32[768]{0:T(1024)} %param.29) | copy-start | bytes 9220
  173.2 45.8 %copy-start.23 = (f32[768]{0:T(1024)S(1)}, f32[768]{0:T(1024)}, u32[]{:S(2)}) copy-start(f32[768]{0:T(1024)} %param.30) | copy-start | bytes 9220
  173.2 45.8 %copy-start.35 = (f32[768]{0:T(1024)S(1)}, f32[768]{0:T(1024)}, u32[]{:S(2)}) copy-start(f32[768]{0:T(1024)} %param.31) | copy-start | bytes 9220
  173.2 54.8 %all-gather.13.cloned.1.call-start = ((), (), s32[]{:S(2)}) async-start(), calls=%async_computation.11 | async-start | bytes 1769472 | tf_op jit(solution)/shard_map/all_gather | solution.py:149
  173.8 101.6 %copy-start.41 = (f32[768]{0:T(1024)S(1)}, f32[768]{0:T(1024)}, u32[]{:S(2)}) copy-start(f32[768]{0:T(1024)} %param.33) | copy-start | bytes 9220
  173.8 101.6 %all-gather.11.cloned.1.call-start = ((), (), s32[]{:S(2)}) async-start(), calls=%async_computation.10 | async-start | bytes 3932160 | tf_op jit(solution)/shard_map/all_gather | solution.py:16
  221.6 72.8 %all-gather.15.cloned.1.call-start = ((), (), s32[]{:S(2)}) async-start(), calls=%async_computation.12 | async-start | bytes 1769472 | tf_op jit(solution)/shard_map/all_gather | solution.py:150
  222.2 110.9 %all-gather.17.cloned.1.call-start = ((), (), s32[]{:S(2)}) async-start(), calls=%async_computation.14 | async-start | bytes 3932160 | tf_op jit(solution)/shard_map/all_gather | solution.py:26
  222.9 171.2 %reduce-scatter.21.cloned.1.call-start = ((), (), s32[]{:S(2)}) async-start(), calls=%async_computation.15 | async-start | bytes 3932160 | tf_op jit(solution)/shard_map/reduce_scatter | solution.py:30
  333.1 12.8 %copy-start.40 = (bf16[768,768]{1,0:T(8,128)(2,1)S(1)}, bf16[768,768]{1,0:T(8,128)(2,1)}, u32[]{:S(2)}) copy-start(bf16[768,768]{1,0:T(8,128)(2,1)} %all-gather.13.cloned.1.call-done) | copy-start | bytes 3538948
  350.0 91.1 %reduce-scatter.19.cloned.1.call-start = ((), (), s32[]{:S(2)}) async-start(), calls=%async_computation.13 | async-start | bytes 3932160 | tf_op jit(solution)/shard_map/reduce_scatter | solution.py:20
  356.8 37.3 %copy-start.4 = (bf16[1,512,768]{2,1,0:T(8,128)(2,1)S(1)}, bf16[1,512,768]{2,1,0:T(8,128)(2,1)}, u32[]{:S(2)}) copy-start(bf16[1,512,768]{2,1,0:T(8,128)(2,1)} %reduce-scatter.17.cloned.1.call-done) | copy-start | bytes 2359300
  356.8 84.2 %copy-start.36 = (f32[768]{0:T(1024)S(1)}, f32[768]{0:T(1024)}, u32[]{:S(2)}) copy-start(f32[768]{0:T(1024)} %param.35) | copy-start | bytes 9220
  356.9 134.8 %all-gather.19.cloned.1.call-start = ((), (), s32[]{:S(2)}) async-start(), calls=%async_computation.16 | async-start | bytes 3932160 | tf_op jit(solution)/shard_map/all_gather | solution.py:26
  447.5 165.3 %reduce-scatter.31.cloned.1.call-start = ((), (), s32[]{:S(2)}) async-start(), calls=%async_computation.23 | async-start | bytes 1769472
  457.5 157.6 %reduce-scatter.29.cloned.1.call-start = ((), (), s32[]{:S(2)}) async-start(), calls=%async_computation.22 | async-start | bytes 589824
  596.3 20.5 %reduce-scatter.27.cloned.1.call-start = ((), (), s32[]{:S(2)}) async-start(), calls=%async_computation.21 | async-start | bytes 1474560
  601.7 6.9 copy-start.7
  601.7 6.9 copy-start.9
  601.7 6.9 copy-start.14
  601.7 27.5 %reduce-scatter.25.cloned.1.call-start = ((), (), s32[]{:S(2)}) async-start(), calls=%async_computation.19 | async-start | bytes 1769472 | tf_op jit(solution)/shard_map/reduce_scatter | solution.py:308
  608.5 68.7 %reduce-scatter.23.cloned.1.call-start = ((), (), s32[]{:S(2)}) async-start(), calls=%async_computation.17 | async-start | bytes 3932160 | tf_op jit(solution)/shard_map/reduce_scatter | solution.py:30
  612.7 64.6 %copy-start.1 = (bf16[1,512,768]{2,1,0:T(8,128)(2,1)S(1)}, bf16[1,512,768]{2,1,0:T(8,128)(2,1)}, u32[]{:S(2)}) copy-start(bf16[1,512,768]{2,1,0:T(8,128)(2,1)} %param.20) | copy-start | bytes 2359300
  612.7 64.6 %copy-start.20 = (f32[768]{0:T(1024)S(1)}, f32[768]{0:T(1024)}, u32[]{:S(2)}) copy-start(f32[768]{0:T(1024)} %copy-done.19) | copy-start | bytes 9220
  612.7 64.6 %copy-start.25 = (f32[768]{0:T(1024)S(1)}, f32[768]{0:T(1024)}, u32[]{:S(2)}) copy-start(f32[768]{0:T(1024)} %param.25) | copy-start | bytes 9220
  612.7 64.6 %copy-start.27 = (f32[512]{0:T(512)S(1)}, f32[512]{0:T(512)}, u32[]{:S(2)}) copy-start(f32[512]{0:T(512)} %copy-done.26) | copy-start | bytes 6148
  612.7 64.6 %copy-start.29 = (f32[512]{0:T(512)S(1)}, f32[512]{0:T(512)}, u32[]{:S(2)}) copy-start(f32[512]{0:T(512)} %copy-done.28) | copy-start | bytes 6148
  612.7 66.6 %copy-start.3 = (f32[1,512,768]{2,1,0:T(8,128)S(1)}, f32[1,512,768]{2,1,0:T(8,128)}, u32[]{:S(2)}) copy-start(f32[1,512,768]{2,1,0:T(8,128)} %copy-done.2) | copy-start | bytes 4718596
  612.7 145.1 %all-reduce.9.cloned.1.call-start = ((), (), s32[]{:S(2)}) async-start(), calls=%async_computation.24 | async-start | bytes 3538944 | tf_op jit(solution)/shard_map/psum | solution.py:323
  629.3 244.1 %all-reduce.7.cloned.1.call-start = ((), (), s32[]{:S(2)}) async-start(), calls=%async_computation.18 | async-start | bytes 1548288 | tf_op jit(solution)/shard_map/psum | solution.py:325
  679.3 9.9 %copy-start.38 = (u32[32]{0:T(128)S(1)}, u32[32]{0:T(128)}, u32[]{:S(2)}) copy-start(u32[32]{0:T(128)} %constant.160) | copy-start | bytes 388
  682.5 10.5 %copy-start.37 = (f32[768]{0:T(1024)S(1)}, f32[768]{0:T(1024)}, u32[]{:S(2)}) copy-start(f32[768]{0:T(1024)} %get-tuple-element.411) | copy-start | bytes 9220
  686.9 3.5 collective-permute-start
  693.0 72.0 %copy-start.30 = (f32[768]{0:T(1024)S(1)}, f32[768]{0:T(1024)}, u32[]{:S(2)}) copy-start(f32[768]{0:T(1024)} %get-tuple-element.331) | copy-start | bytes 9220
  693.0 72.0 %copy-start.31 = (f32[768]{0:T(1024)S(1)}, f32[768]{0:T(1024)}, u32[]{:S(2)}) copy-start(f32[768]{0:T(1024)} %get-tuple-element.341) | copy-start | bytes 9220
  693.0 72.0 %copy-start.32 = (f32[768]{0:T(1024)S(1)}, f32[768]{0:T(1024)}, u32[]{:S(2)}) copy-start(f32[768]{0:T(1024)} %get-tuple-element.393) | copy-start | bytes 9220
  693.0 72.0 %copy-start.33 = (f32[768]{0:T(1024)S(1)}, f32[768]{0:T(1024)}, u32[]{:S(2)}) copy-start(f32[768]{0:T(1024)} %get-tuple-element.405) | copy-start | bytes 9220
  (22 other events, 83.7 us)
Sparse Core Ops, SparseCore 0:
  9.6 12.4 all-gather.20
  26.0 45.1 all-gather.8
  173.4 43.9 reduce-scatter.16
  218.8 9.1 all-gather.12
  230.3 45.1 all-gather.10
  276.8 9.2 all-gather.14
  287.9 45.1 all-gather.16
  350.1 43.9 reduce-scatter.20
  397.1 43.9 reduce-scatter.18
  447.6 43.9 all-gather.18
  494.4 8.6 reduce-scatter.30
  596.4 7.6 reduce-scatter.28
  606.9 9.6 reduce-scatter.26
  619.4 9.8 reduce-scatter.24
  632.1 45.1 reduce-scatter.22
  680.9 76.8 all-reduce.8
  764.4 108.9 all-reduce.6
where the time goes:
time: 892 us; the launch traced here: 882 us
  waiting for transfers between devices  480 us (54%)
  matrix products  196 us (22%)
  other arithmetic  72.5 us (8%)
  blocking collectives  67.1 us (8%)
  local copies, waits for them, and re-layouts  33.4 us (4%)
  between operations  16.1 us (2%)
  loops' own time  14.2 us (2%)
    all_gather x2, waiting for transfers between devices, gather_rows(): return lax.all_gather(values, 'row', axis=1, tiled=True)  88.2 us
    reduce_scatter x2, waiting for transfers between devices, scatter_rows(): lax.psum_scatter(values.astype(jnp.bfloat16), 'row', scatter_dimension=1,...  87.5 us
    reduce_scatter x2, waiting for transfers between devices, scatter_grads(): lax.psum_scatter(values.astype(jnp.bfloat16), 'row', scatter_dimension=1,...  85.2 us
    all_gather x2, waiting for transfers between devices, gather_grads(): return lax.all_gather(values, 'row', axis=1, tiled=True)  72.8 us
    psum x1, waiting for transfers between devices, body(): lax.psum(blocks[4].astype(jnp.bfloat16), ('dp', 'row')).astype(jnp.float32)  68.4 us
    psum x1, waiting for transfers between devices, body(): lax.psum(blocks[3].astype(jnp.bfloat16), 'dp').astype(jnp.float32)  46.5 us
    psum x1, blocking collectives, body(): lax.psum((ln1_gain_part, ln1_bias_part, jnp.sum(grad_hidden1, axis=(0, 1)...  40 us
    dot_general x8, matrix products, one_block(): jnp.einsum('qhd,khd->hqk', query_blk, key_rows, preferred_element_type=jn...  31.4 us
  transfers between devices with their start and end apart: 18, of which 13 were waited for; matrix products, arithmetic and copies ran while one was open for 20% of the time, Pallas kernels for 0%

commit v1 on v0

--- a/solution.py
+++ b/solution.py
@@ -6,6 +6,10 @@
 HD = 64
 norm_eps = 1e-05
 masked_score = -1e30
+
+
+def _settle_sample(a0):
+    return jnp.sum(lax.all_gather(a0, "dp"), 0)
 
 
 def gelu_exact(values):
@@ -320,7 +324,7 @@
         lax.psum(blocks[0].astype(jnp.bfloat16), "dp").astype(jnp.float32),
         lax.psum(blocks[1].astype(jnp.bfloat16), "dp").astype(jnp.float32),
         lax.psum(blocks[2].astype(jnp.bfloat16), "dp").astype(jnp.float32),
-        lax.psum(blocks[3].astype(jnp.bfloat16), "dp").astype(jnp.float32),
+        _settle_sample(blocks[3].astype(jnp.bfloat16)).astype(jnp.float32),
     )
     table_block = lax.psum(blocks[4].astype(jnp.bfloat16), ("dp", "row")).astype(jnp.float32)
     return (

time: 892 us -> 923 us (1.035)
  waiting for transfers between devices: 480 us -> 502 us
    all_gather x0 -> x1, waiting for transfers between devices: none -> 19 us  [_settle_sample(): return jnp.sum(lax.all_gather(a0, 'dp'), 0)]
    unnamed x93 -> x83, local copies, waits for them, and re-layouts: 23.4 us -> 21.7 us
  transfers between devices with their start and end apart: 18 -> 19, of which waited for: 13 -> 14; matrix products, arithmetic and copies ran while one was open for 20% -> 20% of each run, Pallas kernels for 0% -> 0%
where the time goes in v1:
time: 923 us; the launch traced here: 913 us
  waiting for transfers between devices  502 us (54%)
  matrix products  197 us (21%)
  other arithmetic  76.2 us (8%)
  blocking collectives  67.5 us (7%)
  local copies, waits for them, and re-layouts  36.7 us (4%)
  between operations  16.7 us (2%)
  loops' own time  14 us (2%)
    all_gather x2, waiting for transfers between devices, gather_rows(): return lax.all_gather(values, 'row', axis=1, tiled=True)  88.2 us
    reduce_scatter x2, waiting for transfers between devices, scatter_rows(): lax.psum_scatter(values.astype(jnp.bfloat16), 'row', scatter_dimension=1,...  87.5 us
    reduce_scatter x2, waiting for transfers between devices, scatter_grads(): lax.psum_scatter(values.astype(jnp.bfloat16), 'row', scatter_dimension=1,...  84.9 us
    all_gather x2, waiting for transfers between devices, gather_grads(): return lax.all_gather(values, 'row', axis=1, tiled=True)  72.7 us
    psum x1, waiting for transfers between devices, body(): lax.psum(blocks[4].astype(jnp.bfloat16), ('dp', 'row')).astype(jnp.float32)  68.7 us
    psum x1, waiting for transfers between devices, body(): lax.psum(blocks[0].astype(jnp.bfloat16), 'dp').astype(jnp.float32)  50.3 us
    psum x1, blocking collectives, body(): lax.psum((ln1_gain_part, ln1_bias_part, jnp.sum(grad_hidden1, axis=(0, 1)...  40.8 us
    dot_general x8, matrix products, one_block(): jnp.einsum('qhd,khd->hqk', query_blk, key_rows, preferred_element_type=jn...  31.4 us
  transfers between devices with their start and end apart: 19, of which 14 were waited for; matrix products, arithmetic and copies ran while one was open for 20% of the time, Pallas kernels for 0%

profile of v1, /device:TPU:0, one launch (start us, length us, event | category | flops | bytes accessed | tf_op | source)
XLA Modules:
  0.0 913.3 jit_solution(2514501907001744736)
XLA Ops:
  8.7 13.4 %all-gather.25.cloned.1.call-done = bf16[2,500,768]{2,1,0:T(8,128)(2,1)} async-done(((bf16[1,500,768]{2,1,0:T(8,128)(2,1)}), bf16[2,500,768]{2,1,0:T(8,128)(2,1)}) %all-gather.25.cloned.1.call-update) | async-done | bytes 1536016 | tf_op jit(solution)/shard_map/all_gather | solution.py:155
  30.4 40.8 %all-gather.11.cloned.1.call-done = bf16[1,2048,768]{2,1,0:T(8,128)(2,1)} async-done(((bf16[1,512,768]{2,1,0:T(8,128)(2,1)}), bf16[1,2048,768]{2,1,0:T(8,128)(2,1)}) %all-gather.11.cloned.1.call-update) | async-done | bytes 3145744 | tf_op jit(solution)/shard_map/all_gather | solution.py:20
  76.6 91.9 %while.50 = (s32[]{:T(128)}, f32[4,512,3,64]{1,3,2,0:T(8,128)}, f32[4,3,512]{2,1,0:T(4,128)S(1)}, s32[4]{0:T(128)S(1)}, s32[]{:T(128)}, /*index=5*/bf16[2048,3,6...) while((s32[]{:T(128)}, f32[4,512,3,64]{1,3,2,0:T(8,128)}, ...), condition=%wide.region_5.6_spmd.clone.clone.clone, body=%wide.region_2.5_spmd.clone.clone.sunk.clone | while | flops 845153280 | bytes 47315148 | solution.py:80
  79.3 6.0 fusion.182
  85.3 6.8 fusion.183
  92.1 7.4 fusion.184
  102.3 6.0 fusion.182
  108.3 6.8 fusion.183
  115.1 7.4 fusion.184
  125.2 6.0 fusion.182
  131.2 6.8 fusion.183
  138.1 7.4 fusion.184
  148.2 6.0 fusion.182
  154.2 6.8 fusion.183
  161.1 7.4 fusion.184
  174.4 43.2 %reduce-scatter.17.cloned.1.call-done = bf16[1,512,768]{2,1,0:T(8,128)(2,1)} async-done(((bf16[1,2048,768]{2,1,0:T(8,128)(2,1)}), bf16[1,512,768]{2,1,0:T(8,128)(2,1)}) %reduce-scatter.17.cloned.1.call-update) | async-done | bytes 786448 | tf_op jit(solution)/shard_map/reduce_scatter | solution.py:24
  223.2 5.1 all-gather.15.cloned.1.call-done
  228.3 47.4 %all-gather.13.cloned.1.call-done = bf16[1,2048,768]{2,1,0:T(8,128)(2,1)} async-done(((bf16[1,512,768]{2,1,0:T(8,128)(2,1)}), bf16[1,2048,768]{2,1,0:T(8,128)(2,1)}) %all-gather.13.cloned.1.call-update) | async-done | bytes 3145744 | tf_op jit(solution)/shard_map/all_gather | solution.py:20
  275.7 19.0 %multiply_convert_fusion.1 = (bf16[2048,768]{1,0:T(8,128)(2,1)}, f32[2048,768]{1,0:T(8,128)}, f32[2048,768]{1,0:T(8,128)}) fusion(f32[768]{0:T(1024)S(1)} %copy-done.37, bf16[768,768]{1,0:T(8,128)(2,1)} %all-gather.15.cloned.1.call-done, bf16[1,2048,768]{2,1,0:T(8,128)(2,1)} %all-gather.13.cloned.1.call-done), kind=kOutput, calls=%fused_computation.54 | convolution fusion | flops 2519728128 | bytes 20057088 | tf_op jit(solution)/shard_map/std,df->stf/dot_general | solution.py:187
  294.7 38.6 %all-gather.19.cloned.1.call-done = bf16[1,2048,768]{2,1,0:T(8,128)(2,1)} async-done(((bf16[1,512,768]{2,1,0:T(8,128)(2,1)}), bf16[1,2048,768]{2,1,0:T(8,128)(2,1)}) %all-gather.19.cloned.1.call-update) | async-done | bytes 3145744 | tf_op jit(solution)/shard_map/all_gather | solution.py:30
  333.4 11.2 %fusion.112 = (f32[768]{0:T(1024)}, bf16[2048,768]{1,0:T(8,128)(2,1)S(1)}) fusion(f32[2048,768]{1,0:T(8,128)} %get-tuple-element.369, bf16[768,768]{1,0:T(8,128)(2,1)} %all-gather.17.cloned.1.call-done, bf16[1,2048,768]{2,1,0:T(8,128)(2,1)} %all-gather.19.cloned.1.call-done, f32[2048,768]{1,0:T(8,128)} %get-tuple-element.381, f32[768]{0:T(1024)S(1)} %copy-done.37), kind=kOutput, calls=%fused_computation.153 | convolution fusion | flops 2441084160 | bytes 20060160 | tf_op jit(solution)/shard_map/std,df->stf/dot_general | solution.py:233
  346.2 4.0 fusion.66
  350.7 6.6 fusion.65
  357.4 37.0 %reduce-scatter.21.cloned.1.call-done = bf16[1,512,768]{2,1,0:T(8,128)(2,1)} async-done(((bf16[1,2048,768]{2,1,0:T(8,128)(2,1)}), bf16[1,512,768]{2,1,0:T(8,128)(2,1)}) %reduce-scatter.21.cloned.1.call-update) | async-done | bytes 786448 | tf_op jit(solution)/shard_map/reduce_scatter | solution.py:34
  397.1 44.2 %reduce-scatter.19.cloned.1.call-done = bf16[1,512,768]{2,1,0:T(8,128)(2,1)} async-done(((bf16[1,2048,768]{2,1,0:T(8,128)(2,1)}), bf16[1,512,768]{2,1,0:T(8,128)(2,1)}) %reduce-scatter.19.cloned.1.call-update) | async-done | bytes 786448 | tf_op jit(solution)/shard_map/reduce_scatter | solution.py:24
  441.3 4.2 fusion.108
  448.7 6.5 fusion.100
  457.8 34.1 %all-gather.21.cloned.1.call-done = bf16[1,2048,768]{2,1,0:T(8,128)(2,1)} async-done(((bf16[1,512,768]{2,1,0:T(8,128)(2,1)}), bf16[1,2048,768]{2,1,0:T(8,128)(2,1)}) %all-gather.21.cloned.1.call-update) | async-done | bytes 3145744 | tf_op jit(solution)/shard_map/all_gather | solution.py:30
  501.5 87.6 %while.51 = (s32[]{:T(128)}, f32[2048,3,64]{0,2,1:T(8,128)S(1)}, f32[2048,3,64]{0,2,1:T(8,128)}, bf16[4,512,3,64]{1,3,2,0:T(8,128)(2,1)}, s32[4]{0:T(128)S(1)}, ...) while((s32[]{:T(128)}, f32[2048,3,64]{0,2,1:T(8,128)S(1)}, ...), condition=%wide.region_15.16_spmd.clone.clone.clone, body=%wide.region_14.15_spmd.clone.clone.sunk.clone | while | flops 2048887296 | bytes 79087952 | solution.py:125
  508.2 5.8 fusion.198
  514.0 5.6 multiply_convert_fusion.5
  529.5 6.4 fusion.198
  535.9 5.6 multiply_convert_fusion.5
  551.5 6.4 fusion.198
  557.9 5.6 multiply_convert_fusion.5
  573.4 6.4 fusion.198
  579.8 5.6 multiply_convert_fusion.5
  601.5 6.7 fusion.92
  608.2 5.2 fusion.67
  619.7 9.1 reduce-scatter.25.cloned.1.call-done
  628.9 47.9 %reduce-scatter.23.cloned.1.call-done = bf16[1,512,768]{2,1,0:T(8,128)(2,1)} async-done(((bf16[1,2048,768]{2,1,0:T(8,128)(2,1)}), bf16[1,512,768]{2,1,0:T(8,128)(2,1)}) %reduce-scatter.23.cloned.1.call-update) | async-done | bytes 786448 | tf_op jit(solution)/shard_map/reduce_scatter | solution.py:34
  682.0 4.4 fusion.4
  692.5 17.9 %psum.86 = f32[768]{0:T(1024)} all-reduce(f32[768]{0:T(1024)S(1)} %copy-done.33), channel_id=1, replica_groups=mesh['dp'=4,'row'=4,'col'=2] {'dp','col'}, use_global_device_ids=true, to_apply=%region_39.40 | all-reduce | flops 768 | bytes 6144 | tf_op jit(solution)/shard_map/psum | solution.py:303
  710.4 19.0 %all-gather.23.cloned.1.call-done = bf16[1536,768]{0,1:T(8,128)(2,1)} async-done(((bf16[384,768]{0,1:T(8,128)(2,1)}), bf16[1536,768]{0,1:T(8,128)(2,1)}) %all-gather.23.cloned.1.call-update) | async-done | bytes 2359312 | tf_op jit(solution)/shard_map/all_gather | solution.py:12
  729.4 4.1 reshape.476
  738.1 50.3 %all-reduce.9.cloned.1.call-done = (bf16[384,3,192]{0,2,1:T(8,128)(2,1)}, bf16[384,192]{0,1:T(8,128)(2,1)}, bf16[384,768]{1,0:T(8,128)(2,1)}) async-done(((bf16[384,3,192]{0,2,1:T(8,128)(2,1)}, bf16[384,192]{0,1:T(8,128)(2,1)}, bf16[384,768]{1,0:T(8,128)(2,1)}), (bf16[384,3,192]{0,2,1:T(8,128)(2,1)}, bf16[384,192]{0,1:T(8,128)(2,1)}, bf16[384,768]{1,0:T(8,128)(2,1)})) %all-reduce.9.cloned.1.call-update) | async-done | bytes 1179664 | tf_op jit(solution)/shard_map/psum | solution.py:324
  794.2 40.8 %all-reduce.2 = (f32[768]{0:T(1024)}, f32[768]{0:T(1024)}, f32[768]{0:T(1024)}, f32[768]{0:T(1024)}, f32[768]{0:T(1024)}, /*index=5*/f32[768]{0:T(1024)}) all-reduce(f32[768]{0:T(1024)S(1)} %get-tuple-element.305, f32[768]{0:T(1024)S(1)} %get-tuple-element.314, ...), channel_id=1, replica_groups=mesh['dp'=4,'row'=4,'col'=2] {'dp','row','col'}, use_global_device_ids=true, to_apply=%region_23.24 | all-reduce | flops 4608 | bytes 36864 | tf_op jit(solution)/shard_map/psum | solution.py:292
  834.9 68.7 %all-reduce.7.cloned.1.call-done = bf16[500,768]{1,0:T(8,128)(2,1)} async-done(((bf16[500,768]{1,0:T(8,128)(2,1)}), bf16[500,768]{1,0:T(8,128)(2,1)}) %all-reduce.7.cloned.1.call-update) | async-done | bytes 768016 | tf_op jit(solution)/shard_map/psum | solution.py:329
  (262 shorter events, 124.8 us)
Async XLA Ops:
  7.2 17.0 %copy-start = (bf16[1,512,768]{2,1,0:T(8,128)(2,1)S(1)}, bf16[1,512,768]{2,1,0:T(8,128)(2,1)}, u32[]{:S(2)}) copy-start(bf16[1,512,768]{2,1,0:T(8,128)(2,1)} %param.20) | copy-start | bytes 2359300
  7.2 17.4 %copy-start.20 = (f32[768]{0:T(1024)S(1)}, f32[768]{0:T(1024)}, u32[]{:S(2)}) copy-start(f32[768]{0:T(1024)} %param.25) | copy-start | bytes 9220
  7.2 17.4 %copy-start.30 = (f32[768]{0:T(1024)S(1)}, f32[768]{0:T(1024)}, u32[]{:S(2)}) copy-start(f32[768]{0:T(1024)} %param.26) | copy-start | bytes 9220
  7.2 14.9 %all-gather.25.cloned.1.call-start = ((), (), s32[]{:S(2)}) async-start(), calls=%async_computation.21 | async-start | bytes 2322432 | tf_op jit(solution)/shard_map/all_gather | solution.py:155
  7.9 63.2 %all-gather.11.cloned.1.call-start = ((), (), s32[]{:S(2)}) async-start(), calls=%async_computation.8 | async-start | bytes 3932160 | tf_op jit(solution)/shard_map/all_gather | solution.py:20
  8.7 17.3 %copy-start.17 = (bf16[384,192]{0,1:T(8,128)(2,1)S(1)}, bf16[384,192]{0,1:T(8,128)(2,1)}, u32[]{:S(2)}) copy-start(bf16[384,192]{0,1:T(8,128)(2,1)} %param.28) | copy-start | bytes 442372
  24.1 417.2 %copy-start.15 = (f32[768]{0:T(1024)}, f32[768]{0:T(1024)S(1)}, u32[]{:S(2)}) copy-start(f32[768]{0:T(1024)S(1)} %convolution_reduce_fusion) | copy-start | bytes 9220
  24.6 50.5 %copy-start.22 = (f32[512]{0:T(512)}, f32[512]{0:T(512)S(1)}, u32[]{:S(2)}) copy-start(f32[512]{0:T(512)S(1)} %get-tuple-element.379) | copy-start | bytes 6148
  24.6 50.5 %copy-start.24 = (f32[512]{0:T(512)}, f32[512]{0:T(512)S(1)}, u32[]{:S(2)}) copy-start(f32[512]{0:T(512)S(1)} %get-tuple-element.380) | copy-start | bytes 6148
  25.9 191.7 %reduce-scatter.17.cloned.1.call-start = ((), (), s32[]{:S(2)}) async-start(), calls=%async_computation.9 | async-start | bytes 3932160 | tf_op jit(solution)/shard_map/reduce_scatter | solution.py:24
  30.4 44.7 %copy-start.11 = (bf16[768,3,192]{0,2,1:T(8,128)(2,1)}, bf16[768,3,192]{0,2,1:T(8,128)(2,1)S(1)}, u32[]{:S(2)}) copy-start(bf16[768,3,192]{0,2,1:T(8,128)(2,1)S(1)} %all_gather.35) | copy-start | bytes 2654212
  108.3 6.8 copy-start.12
  154.2 6.8 copy-start.12
  173.5 44.1 %copy-start.18 = (f32[768]{0:T(1024)S(1)}, f32[768]{0:T(1024)}, u32[]{:S(2)}) copy-start(f32[768]{0:T(1024)} %param.29) | copy-start | bytes 9220
  173.5 45.8 %copy-start.19 = (f32[768]{0:T(1024)S(1)}, f32[768]{0:T(1024)}, u32[]{:S(2)}) copy-start(f32[768]{0:T(1024)} %param.30) | copy-start | bytes 9220
  173.5 45.8 %copy-start.31 = (f32[768]{0:T(1024)S(1)}, f32[768]{0:T(1024)}, u32[]{:S(2)}) copy-start(f32[768]{0:T(1024)} %param.31) | copy-start | bytes 9220
  173.5 54.7 %all-gather.15.cloned.1.call-start = ((), (), s32[]{:S(2)}) async-start(), calls=%async_computation.11 | async-start | bytes 1769472 | tf_op jit(solution)/shard_map/all_gather | solution.py:153
  174.1 101.6 %copy-start.37 = (f32[768]{0:T(1024)S(1)}, f32[768]{0:T(1024)}, u32[]{:S(2)}) copy-start(f32[768]{0:T(1024)} %param.33) | copy-start | bytes 9220
  174.1 101.6 %all-gather.13.cloned.1.call-start = ((), (), s32[]{:S(2)}) async-start(), calls=%async_computation.10 | async-start | bytes 3932160 | tf_op jit(solution)/shard_map/all_gather | solution.py:20
  221.8 72.9 %all-gather.17.cloned.1.call-start = ((), (), s32[]{:S(2)}) async-start(), calls=%async_computation.12 | async-start | bytes 1769472 | tf_op jit(solution)/shard_map/all_gather | solution.py:154
  222.4 111.0 %all-gather.19.cloned.1.call-start = ((), (), s32[]{:S(2)}) async-start(), calls=%async_computation.14 | async-start | bytes 3932160 | tf_op jit(solution)/shard_map/all_gather | solution.py:30
  223.2 171.2 %reduce-scatter.21.cloned.1.call-start = ((), (), s32[]{:S(2)}) async-start(), calls=%async_computation.15 | async-start | bytes 3932160 | tf_op jit(solution)/shard_map/reduce_scatter | solution.py:34
  333.4 12.8 %copy-start.36 = (bf16[768,768]{1,0:T(8,128)(2,1)S(1)}, bf16[768,768]{1,0:T(8,128)(2,1)}, u32[]{:S(2)}) copy-start(bf16[768,768]{1,0:T(8,128)(2,1)} %all-gather.15.cloned.1.call-done) | copy-start | bytes 3538948
  350.2 91.1 %reduce-scatter.19.cloned.1.call-start = ((), (), s32[]{:S(2)}) async-start(), calls=%async_computation.13 | async-start | bytes 3932160 | tf_op jit(solution)/shard_map/reduce_scatter | solution.py:24
  357.3 37.1 %copy-start.4 = (bf16[1,512,768]{2,1,0:T(8,128)(2,1)S(1)}, bf16[1,512,768]{2,1,0:T(8,128)(2,1)}, u32[]{:S(2)}) copy-start(bf16[1,512,768]{2,1,0:T(8,128)(2,1)} %reduce-scatter.17.cloned.1.call-done) | copy-start | bytes 2359300
  357.3 84.0 %copy-start.32 = (f32[768]{0:T(1024)S(1)}, f32[768]{0:T(1024)}, u32[]{:S(2)}) copy-start(f32[768]{0:T(1024)} %param.35) | copy-start | bytes 9220
  357.3 134.5 %all-gather.21.cloned.1.call-start = ((), (), s32[]{:S(2)}) async-start(), calls=%async_computation.16 | async-start | bytes 3932160 | tf_op jit(solution)/shard_map/all_gather | solution.py:30
  447.7 165.9 %reduce-scatter.31.cloned.1.call-start = ((), (), s32[]{:S(2)}) async-start(), calls=%async_computation.24 | async-start | bytes 1769472
  457.7 158.3 %reduce-scatter.29.cloned.1.call-start = ((), (), s32[]{:S(2)}) async-start(), calls=%async_computation.23 | async-start | bytes 589824
  595.8 21.9 %reduce-scatter.27.cloned.1.call-start = ((), (), s32[]{:S(2)}) async-start(), calls=%async_computation.22 | async-start | bytes 1474560
  601.5 27.3 %reduce-scatter.25.cloned.1.call-start = ((), (), s32[]{:S(2)}) async-start(), calls=%async_computation.19 | async-start | bytes 1769472 | tf_op jit(solution)/shard_map/reduce_scatter | solution.py:312
  608.2 68.6 %reduce-scatter.23.cloned.1.call-start = ((), (), s32[]{:S(2)}) async-start(), calls=%async_computation.17 | async-start | bytes 3932160 | tf_op jit(solution)/shard_map/reduce_scatter | solution.py:34
  613.5 63.3 %copy-start.1 = (bf16[1,512,768]{2,1,0:T(8,128)(2,1)S(1)}, bf16[1,512,768]{2,1,0:T(8,128)(2,1)}, u32[]{:S(2)}) copy-start(bf16[1,512,768]{2,1,0:T(8,128)(2,1)} %param.20) | copy-start | bytes 2359300
  613.5 63.3 %copy-start.16 = (f32[768]{0:T(1024)S(1)}, f32[768]{0:T(1024)}, u32[]{:S(2)}) copy-start(f32[768]{0:T(1024)} %copy-done.15) | copy-start | bytes 9220
  613.5 63.3 %copy-start.21 = (f32[768]{0:T(1024)S(1)}, f32[768]{0:T(1024)}, u32[]{:S(2)}) copy-start(f32[768]{0:T(1024)} %param.25) | copy-start | bytes 9220
  613.5 63.3 %copy-start.23 = (f32[512]{0:T(512)S(1)}, f32[512]{0:T(512)}, u32[]{:S(2)}) copy-start(f32[512]{0:T(512)} %copy-done.22) | copy-start | bytes 6148
  613.5 63.3 %copy-start.25 = (f32[512]{0:T(512)S(1)}, f32[512]{0:T(512)}, u32[]{:S(2)}) copy-start(f32[512]{0:T(512)} %copy-done.24) | copy-start | bytes 6148
  613.5 65.3 %copy-start.3 = (f32[1,512,768]{2,1,0:T(8,128)S(1)}, f32[1,512,768]{2,1,0:T(8,128)}, u32[]{:S(2)}) copy-start(f32[1,512,768]{2,1,0:T(8,128)} %copy-done.2) | copy-start | bytes 4718596
  613.6 115.9 %all-gather.23.cloned.1.call-start = ((), (), s32[]{:S(2)}) async-start(), calls=%async_computation.20 | async-start | bytes 2949120 | tf_op jit(solution)/shard_map/all_gather | solution.py:12
  615.9 172.4 %all-reduce.9.cloned.1.call-start = ((), (), s32[]{:S(2)}) async-start(), calls=%async_computation.25 | async-start | bytes 2359296 | tf_op jit(solution)/shard_map/psum | solution.py:324
  628.8 274.9 %all-reduce.7.cloned.1.call-start = ((), (), s32[]{:S(2)}) async-start(), calls=%async_computation.18 | async-start | bytes 1548288 | tf_op jit(solution)/shard_map/psum | solution.py:329
  678.8 9.9 %copy-start.34 = (u32[32]{0:T(128)S(1)}, u32[32]{0:T(128)}, u32[]{:S(2)}) copy-start(u32[32]{0:T(128)} %constant.162) | copy-start | bytes 388
  682.0 10.5 %copy-start.33 = (f32[768]{0:T(1024)S(1)}, f32[768]{0:T(1024)}, u32[]{:S(2)}) copy-start(f32[768]{0:T(1024)} %get-tuple-element.382) | copy-start | bytes 9220
  686.4 3.5 collective-permute-start
  736.7 57.4 %copy-start.26 = (f32[768]{0:T(1024)S(1)}, f32[768]{0:T(1024)}, u32[]{:S(2)}) copy-start(f32[768]{0:T(1024)} %get-tuple-element.303) | copy-start | bytes 9220
  736.8 57.4 %copy-start.27 = (f32[768]{0:T(1024)S(1)}, f32[768]{0:T(1024)}, u32[]{:S(2)}) copy-start(f32[768]{0:T(1024)} %get-tuple-element.313) | copy-start | bytes 9220
  736.8 57.4 %copy-start.28 = (f32[768]{0:T(1024)S(1)}, f32[768]{0:T(1024)}, u32[]{:S(2)}) copy-start(f32[768]{0:T(1024)} %get-tuple-element.364) | copy-start | bytes 9220
  736.8 57.4 %copy-start.29 = (f32[768]{0:T(1024)S(1)}, f32[768]{0:T(1024)}, u32[]{:S(2)}) copy-start(f32[768]{0:T(1024)} %get-tuple-element.376) | copy-start | bytes 9220
  (22 other events, 93.4 us)
Sparse Core Ops, SparseCore 0:
  9.6 12.4 all-gather.24
  26.0 45.1 all-gather.10
  173.7 43.9 reduce-scatter.16
  219.0 9.2 all-gather.14
  230.5 45.1 all-gather.12
  277.1 9.2 all-gather.16
  288.2 45.1 all-gather.18
  350.4 43.9 reduce-scatter.20
  397.4 43.9 reduce-scatter.18
  447.8 43.9 all-gather.20
  494.6 8.6 reduce-scatter.30
  596.0 7.6 reduce-scatter.28
  606.5 9.6 reduce-scatter.26
  618.9 9.8 reduce-scatter.24
  631.6 45.1 reduce-scatter.22
  678.8 50.5 all-gather.22
  733.0 55.3 all-reduce.8
  794.1 109.5 all-reduce.6
